TPU v7x, 128 devices: a whole 4x4x4 slice. The times are simulated.
128 devices in a mesh: row: 16 (over y, x), col: 8 (over z, core).
Axes of the slice: x: 4, y: 4, z: 4, core: 2. Of those that a mesh axis runs over, the one named last changes fastest.
Arguments:
- three_centre: float32 [16, 1024, 18432], P('row', None, 'col'), may hold values from -6 to 6
- occupied: float32 [16, 1024, 128], P('row'), may hold values from -0.1875 to 0.1875
- virtual: float32 [16, 1024, 128], P('row'), may hold values from -0.00390625 to 0.00390625
- tile_map: int32 [16, 144], P('row', 'col'), may hold values from 0 to 1, as said below
Outputs:
- polarizability: float32 [18432, 18432], P('row', 'col')
Inputs may be any that keep to these rules, and one draw needn't show every extreme that they name: `tile_map`: 0 or 1; the share of ones differs from orbital to orbital.
All inputs are finite; a program needn't handle non-finite values.
Results may differ from a plain program's by a relative error of at most 0.000071.
Values sent between devices are 32-bit elements; how exact they have to be, the bound alone decides.
A program may use at most 128 MiB of HBM per device.

v0:
```python
import jax
import jax.numpy as jnp
from jax import lax
from jax.sharding import PartitionSpec as P

AB = 128


exact_precision = lax.Precision.HIGHEST


def apply_keep(tensor, tile_map):
    row_count, blocks = tile_map.shape
    keep_factor = jnp.broadcast_to(
        tile_map.astype(jnp.float32)[:, :, None], (row_count, blocks, AB)
    )
    return tensor * keep_factor.reshape(row_count, 1, blocks * AB)


def contract(density, tensor):
    product = jnp.einsum("mnl,mnp->mlp", density, tensor, precision=exact_precision)
    return product.reshape(product.shape[0] * product.shape[1], product.shape[2])


def pair_product(left_rows, right_rows):
    return lax.dot_general(
        left_rows,
        right_rows,
        (((0,), (0,)), ((), ())),
        precision=exact_precision,
        preferred_element_type=jnp.float32,
    )


def body(three_centre, occupied, virtual, tile_map):
    masked = apply_keep(three_centre, tile_map)
    occupied_rows = contract(occupied, masked)
    virtual_rows = contract(virtual, masked)
    occupied_wide = lax.all_gather(occupied_rows, "col", axis=1, tiled=True)
    occupied_here = lax.all_to_all(occupied_wide, "row", split_axis=1, concat_axis=0, tiled=True)
    return pair_product(occupied_here, lax.all_gather(virtual_rows, "row", axis=0, tiled=True))


def solution(mesh):
    return jax.shard_map(
        body,
        mesh=mesh,
        in_specs=(
            P("row", None, "col"),
            P("row", None, None),
            P("row", None, None),
            P("row", "col"),
        ),
        out_specs=P("row", "col"),
        check_vma=False,
    )
```

profile of v0, /device:TPU:1, one launch (start us, length us, event | category | flops | bytes accessed | tf_op | source)
XLA Modules:
  0.0 457.5 jit_solution(5199291999608144530)
XLA Ops:
  6.5 0.0 copy-start
  6.5 0.0 all-gather.3.cloned.1.call-start
  6.5 0.7 convert_bitcast_fusion
  7.3 0.1 broadcast_bitcast_fusion
  7.3 0.3 copy-done
  7.6 0.0 copy-start.2
  7.6 18.2 %fusion.8 = f32[128,2304]{0,1:T(8,128)} fusion(f32[1,1024,2304]{2,1,0:T(8,128)} %param.4, f32[2304]{0:T(1024)S(1)} %broadcast_bitcast_fusion, f32[1,1024,128]{2,1,0:T(8,128)S(1)} %copy-done), kind=kOutput, calls=%fused_computation.8 | convolution fusion | flops 3626237952 | bytes 11150336 | tf_op jit(solution)/shard_map/mnl,mnp->mlp/dot_general | solution.py:21
  25.8 0.0 all-gather.3.cloned.1.call-update
  25.8 0.2 all-gather.5.cloned.1.call-start
  26.1 0.0 copy-done.2
  26.1 18.2 %fusion.11 = f32[128,2304]{0,1:T(8,128)} fusion(f32[1,1024,2304]{2,1,0:T(8,128)} %param.4, f32[2304]{0:T(1024)S(1)} %broadcast_bitcast_fusion, f32[1,1024,128]{2,1,0:T(8,128)S(1)} %copy-done.2), kind=kOutput, calls=%fused_computation.9 | convolution fusion | flops 3626237952 | bytes 11150336 | tf_op jit(solution)/shard_map/mnl,mnp->mlp/dot_general | solution.py:21
  44.2 0.0 all-gather.5.cloned.1.call-update
  44.3 39.7 %all-gather.3.cloned.1.call-done = f32[128,18432]{0,1:T(8,128)} async-done(((f32[128,2304]{0,1:T(8,128)}), f32[128,18432]{0,1:T(8,128)}) %all-gather.3.cloned.1.call-update) | async-done | bytes 9437200 | tf_op jit(solution)/shard_map/all_gather | solution.py:39
  84.0 9.6 %copy.5 = f32[128,16,1152]{2,0,1:T(8,128)} copy(f32[128,16,1152]{0,2,1:T(8,128)} %bitcast.29) | data formatting | bytes 18874368 | tf_op jit(solution)/shard_map/all_to_all | solution.py:40
  93.6 130.1 %all_to_all.19 = f32[128,16,1152]{2,0,1:T(8,128)} all-to-all(f32[128,16,1152]{2,0,1:T(8,128)} %copy.5), channel_id=1, replica_groups=mesh['row'=16,'col'=8] {'row'}, dimensions={1} | all-to-all | bytes 18874368 | tf_op jit(solution)/shard_map/all_to_all | solution.py:40
  223.7 89.0 %all-gather.5.cloned.1.call-done = f32[2048,2304]{0,1:T(8,128)} async-done(((f32[128,2304]{0,1:T(8,128)}), f32[2048,2304]{0,1:T(8,128)}) %all-gather.5.cloned.1.call-update) | async-done | bytes 18874384 | tf_op jit(solution)/shard_map/all_gather | solution.py:41
  312.6 0.0 copy-start.1
  312.6 138.0 %fusion.16 = f32[1152,2304]{1,0:T(8,128)} fusion(f32[2048,1152]{1,0:T(8,128)} %bitcast.30, f32[2048,2304]{0,1:T(8,128)} %all-gather.5.cloned.1.call-done), kind=kOutput, calls=%fused_computation.14 | convolution fusion | flops 65229815808 | bytes 38928384 | tf_op jit(solution)/shard_map/dot_general | solution.py:26
  450.6 0.0 copy-done.1
Async XLA Ops:
  6.5 1.1 copy-start
  6.5 77.4 %all-gather.3.cloned.1.call-start = ((), (), s32[]{:S(2)}) async-start(), calls=%async_computation.1 | async-start | bytes 10616832 | tf_op jit(solution)/shard_map/all_gather | solution.py:39
  7.6 18.5 %copy-start.2 = (f32[1,1024,128]{2,1,0:T(8,128)S(1)}, f32[1,1024,128]{2,1,0:T(8,128)}, u32[]{:S(2)}) copy-start(f32[1,1024,128]{2,1,0:T(8,128)} %param.6) | copy-start | bytes 1572868
  25.8 286.8 %all-gather.5.cloned.1.call-start = ((), (), s32[]{:S(2)}) async-start(), calls=%async_computation.2 | async-start | bytes 20054016 | tf_op jit(solution)/shard_map/all_gather | solution.py:41
  312.6 138.0 %copy-start.1 = (f32[1,1024,128]{2,1,0:T(8,128)S(1)}, f32[1,1024,128]{2,1,0:T(8,128)}, u32[]{:S(2)}) copy-start(f32[1,1024,128]{2,1,0:T(8,128)} %param.5) | copy-start | bytes 1572868
Sparse Core Ops, SparseCore 0:
  26.0 57.9 all-gather.2
  86.1 226.5 all-gather.4
where the time goes:
time: 458 us; the launch traced here: 457 us
  matrix products  174 us (38%)
  blocking collectives  130 us (28%)
  waiting for transfers between devices  129 us (28%)
  between operations  13.4 us (3%)
  local copies, waits for them, and re-layouts  9.94 us (2%)
    dot_general x1, matrix products, pair_product(): lax.dot_general(left_rows, right_rows, (((0,), (0,)), ((), ())), precisio...  138 us
    all_to_all x1, blocking collectives, body(): lax.all_to_all(occupied_wide, 'row', split_axis=1, concat_axis=0, tiled=T...  130 us
    all_gather x1, waiting for transfers between devices, body(): lax.all_gather(virtual_rows, 'row', axis=0, tiled=True)  89 us
    all_gather x1, waiting for transfers between devices, body(): occupied_wide = lax.all_gather(occupied_rows, 'col', axis=1, tiled=True)  39.7 us
    dot_general x2, matrix products, contract(): jnp.einsum('mnl,mnp->mlp', density, tensor, precision=exact_precision)  36.4 us
    all_to_all x1, local copies, waits for them, and re-layouts, body(): lax.all_to_all(occupied_wide, 'row', split_axis=1, concat_axis=0, tiled=T...  9.59 us
  transfers between devices with their start and end apart: 2, of which 2 were waited for; matrix products, arithmetic and copies ran while one was open for 6% of the time, Pallas kernels for 0%

commit v1 on v0

v1 whole, which is shorter than its diff:
```python
import functools

import jax
import jax.numpy as jnp
from jax import lax
from jax.experimental import pallas as pl
from jax.experimental.pallas import tpu as pltpu
from jax.sharding import PartitionSpec as P

MESH = pl.DeviceIdType.MESH
F32, BF16 = jnp.float32, jnp.bfloat16
HALF_BLOCKS = 9
TILES = 16 * HALF_BLOCKS
WIDE = 384
PAIRS = 128
CAPS = (72, 80, 88, 96, TILES)


def place():
    row, col = lax.axis_index("row"), lax.axis_index("col")
    return row // 4, lax.rem(row, 4), col // 2, lax.rem(col, 2)


def device(y, x, z, core):
    return (y * 4 + x, z * 2 + core)


def turn(i, d):
    return lax.rem(i + (d + 4), 4)


def split(x):
    high = x.astype(BF16)
    return high, (x - high.astype(F32)).astype(BF16)


def dot3(ah, al, bh, bl):
    dot = functools.partial(jnp.dot, preferred_element_type=F32)
    return dot(ah, bh) + dot(ah, bl) + dot(al, bh)


def remote(src, dst, send, recv, target):
    return pltpu.make_async_remote_copy(
        src_ref=src, dst_ref=dst, send_sem=send, recv_sem=recv, device_id=target, device_id_type=MESH
    )


def signal(target):
    pl.semaphore_signal(pltpu.get_barrier_semaphore(), inc=1, device_id=target, device_id_type=MESH)


def spread_kernel(
    map_hbm, t_ref, occ_hbm, vir_hbm, v2_ref, op_ref, maps_ref, sums_ref,
    map_ref, occ_ref, vir_ref, tbuf, dh, dl, vbuf, obuf, v1, maps, sums,
    ox, oz, isem, tsem, s1, r1, s2, r2, loc, osend, orecv, ms, mr, ss, sr,
):
    y, x, z, core = place()
    me_row, me_col = y * 4 + x, z * 2 + core
    barrier = pltpu.get_barrier_semaphore()

    loads = [
        pltpu.make_async_copy(t_ref.at[:, pl.ds(i * WIDE, WIDE)], tbuf.at[i], tsem.at[i]) for i in range(6)
    ]
    small = [
        pltpu.make_async_copy(src, dst, isem.at[i])
        for i, (src, dst) in enumerate(((occ_hbm, occ_ref), (vir_hbm, vir_ref), (map_hbm, map_ref)))
    ]
    for load in small + loads:
        load.start()

    for d in (1, 2, 3):
        signal(device(y, turn(x, d), z, core))
        signal(device(turn(y, d), x, z, core))
    for d in range(1, 8):
        signal((me_row, lax.rem(me_col + d, 8)))
    parity = (lax.rem(x, 2), lax.rem(z, 2), lax.rem(y, 2))
    slot = (x // 2, z // 2, y // 2)

    def pair(i):
        return 2 * i + core

    targets = (
        [device(y, 2 * core + i, z, parity[0]) for i in range(2)],
        [device(y, x, pair(i), parity[1]) for i in range(2)],
        [device(pair(i), x, z, parity[2]) for i in range(2)],
    )
    sources = (
        [device(y, pair(i), z, x // 2) for i in range(2)],
        [device(y, x, pair(i), parity[1]) for i in range(2)],
        [device(pair(i), x, z, parity[2]) for i in range(2)],
    )

    def is_me(target):
        return (target[0] == me_row) & (target[1] == me_col)

    for stage in range(3):
        for source in sources[stage]:

            @pl.when(jnp.logical_not(is_me(source)))
            def _():
                signal(source)

    stays = [[is_me(target) for target in line] for line in targets]
    route = (obuf, ox, oz, op_ref)

    def piece(stage, i, q):
        spot = route[stage + 1].at[slot[stage], q]
        recv = orecv.at[stage, slot[stage], q]
        return remote(route[stage].at[i, q], spot, osend.at[stage, i, q], recv, targets[stage][i])

    def piece_start(stage, i, q):
        @pl.when(stays[stage][i])
        def _():
            spot = route[stage + 1].at[slot[stage], q]
            pltpu.make_async_copy(route[stage].at[i, q], spot, orecv.at[stage, slot[stage], q]).start()

        @pl.when(jnp.logical_not(stays[stage][i]))
        def _():
            piece(stage, i, q).start()

    def piece_arrived(stage, i, q):
        spot = route[stage + 1].at[i, q]
        pltpu.make_async_copy(spot, spot, orecv.at[stage, i, q]).wait()

    for part, ref in enumerate((occ_ref, vir_ref)):
        small[part].wait()
        high, low = split(ref[...].T)
        dh[pl.ds(part * PAIRS, PAIRS), :] = high
        dl[pl.ds(part * PAIRS, PAIRS), :] = low

    small[2].wait()
    lane = lax.broadcasted_iota(jnp.int32, (8, 128), 1)
    mine = jnp.zeros((8, 128), jnp.int32)
    for b in range(2 * HALF_BLOCKS):
        mine = jnp.where(lane == b, map_ref[0, b], mine)
    maps[y, x] = mine

    pl.semaphore_wait(barrier, 13 + sum(jnp.where(stay, 0, 1) for line in stays for stay in line))

    told = []
    for d in (1, 2, 3):
        told.append(
            remote(maps.at[y, x], maps.at[y, x], ms.at[0, d - 1], mr.at[0, d - 1], device(y, turn(x, d), z, core))
        )
        told[-1].start()

    first = []
    for h in range(2):
        for q in range(3):
            loads[3 * h + q].wait()

        def chunk(q, _):
            th, tl = split(tbuf[3 * h + q])
            r = dot3(dh[...], dl[...], th, tl)
            for b in range(3):
                keep = map_ref[0, HALF_BLOCKS * h + 3 * q + b].astype(F32)
                cut = slice(b * 128, b * 128 + 128)
                obuf[h, q, :, cut] = r[:PAIRS, cut] * keep
                vbuf[h, 3 * q + b] = r[PAIRS:, cut] * keep
            return 0

        lax.fori_loop(0, 3, chunk, 0)

        if h == 0:
            for copy in told:
                copy.wait_recv()
            for d in (1, 2, 3):
                told.append(
                    remote(maps.at[y], maps.at[y], ms.at[1, d - 1], mr.at[1, d - 1], device(turn(y, d), x, z, core))
                )
                told[-1].start()

        for q in range(3):
            piece_start(0, h, q)

        here = y if h else x
        sends = []
        for d in (1, 2, 3):
            to = turn(here, d)
            copy = remote(
                vbuf.at[h, :, pl.ds(pl.multiple_of(to * 32, 32), 32), :],
                v1.at[h, here],
                s1.at[h, d - 1],
                r1.at[h, d - 1],
                device(to, x, z, core) if h else device(y, to, z, core),
            )
            copy.start()
            sends.append(copy)
        first.append(sends)
        v1[h, here] = vbuf[h, :, pl.ds(pl.multiple_of(here * 32, 32), 32), :]

    for copy in told[3:]:
        copy.wait_recv()
    sums[me_col] = jnp.sum(maps[...].reshape(16, 8, 128), axis=0)
    for d in range(1, 8):
        told.append(
            remote(
                sums.at[me_col], sums.at[me_col], ss.at[d - 1], sr.at[d - 1], (me_row, lax.rem(me_col + d, 8))
            )
        )
        told[-1].start()

    second = []
    for h in range(2):
        for copy in first[h]:
            copy.wait_recv()
        here = x if h else y
        spot = v2_ref.at[1, :, x] if h else v2_ref.at[0, y]
        for d in (1, 2, 3):
            to = turn(here, d)
            copy = remote(
                v1.at[h, :, :, pl.ds(pl.multiple_of(to * 8, 8), 8), :],
                spot,
                s2.at[h, d - 1],
                r2.at[h, d - 1],
                device(y, to, z, core) if h else device(to, x, z, core),
            )
            copy.start()
            second.append(copy)
        copy = pltpu.make_async_copy(
            v1.at[h, :, :, pl.ds(pl.multiple_of(here * 8, 8), 8), :], spot, loc.at[h]
        )
        copy.start()
        second.append(copy)

        for q in range(3):
            for i in range(2):
                piece_arrived(h, i, q)
                piece_start(h + 1, i, q)

    for copy in told[6:]:
        copy.wait_recv()
    maps_ref[...] = maps[...].reshape(16, 8, 128)
    sums_ref[...] = sums[...]
    for copy in told:
        copy.wait_send()
    for i in range(2):
        for q in range(3):
            piece_arrived(2, i, q)
    for copy in second:
        copy.wait()
    for h in range(2):
        for copy in first[h]:
            copy.wait_send()
    for stage in range(3):
        for i in range(2):

            @pl.when(jnp.logical_not(stays[stage][i]))
            def _():
                for q in range(3):
                    piece(stage, i, q).wait_send()


def join_kernel(
    cap, table_hbm, v2_hbm, op_ref, out_ref, table, v2_ref,
    g00, g01, g02, g03, g10, g11, g12, g13, oall, lh, ll, rh, rl, acc,
    p1s, p1r, p2s, p2r, zs, zr, bs, br, loc, osem, isem,
):
    y, x, z, core = place()
    small = [pltpu.make_async_copy(table_hbm, table, isem.at[0]), pltpu.make_async_copy(v2_hbm, v2_ref, isem.at[1])]
    for load in small:
        load.start()
    barrier = pltpu.get_barrier_semaphore()
    got = ((g00, g01, g02, g03), (g10, g11, g12, g13))
    near = (
        device(y, turn(x, 1), z, core), device(y, turn(x, -1), z, core),
        device(turn(y, 1), x, z, core), device(turn(y, -1), x, z, core),
        device(y, x, turn(z, 1), core), device(y, x, turn(z, -1), core),
        device(y, x, z, 1 - core),
    )
    for target in near:
        signal(target)
    pl.semaphore_wait(barrier, len(near))
    x_next, x_last, y_next, y_last, z_next, z_last, twin = near
    sent = []

    def go(make):
        make().start()
        sent.append(make)
        return make

    zslot = (z, turn(z, -1), turn(z, 1), turn(z, 2))
    zcopy, bcopy = {}, {}
    for c in range(3):

        def first(send, recv, n, target, c=c):
            return go(lambda: remote(op_ref.at[:, c], oall.at[c, core, z], send.at[c, n], recv.at[c, n], target))

        zcopy[c, 0] = first(zs, zr, 0, z_next)
        zcopy[c, 1] = first(zs, zr, 1, z_last)
        bcopy[c, 0] = first(bs, br, 0, twin)
        pltpu.make_async_copy(op_ref.at[:, c], oall.at[c, core, z], loc.at[c]).start()

    def relay(c, n, part, target):
        def make():
            spot = oall.at[c, core, zslot[n], part]
            return remote(spot, spot, zs.at[c, n + 1], zr.at[c, n + 1], target)

        zcopy[c, n + 1] = go(make)

    def share(c, n):
        def make():
            spot = oall.at[c, core, zslot[n]]
            return remote(spot, spot, bs.at[c, n], br.at[c, n], twin)

        bcopy[c, n] = go(make)

    def occupied_near(c):
        for n, target in ((1, z_next), (2, z_last)):
            zcopy[c, n - 1]().wait_recv()
            relay(c, n, n - 1, target)
            share(c, n)

    def occupied_far(c):
        zcopy[c, 2]().wait_recv()
        zcopy[c, 3]().wait_recv()
        share(c, 3)

    def left(c):
        pltpu.make_async_copy(op_ref.at[:, c], oall.at[c, core, z], loc.at[c]).wait()
        for n in range(4):
            bcopy[c, n]().wait_recv()

        def rows(g, _):
            for j in range(4):
                t = oall[c, :, :, :, pl.ds(pl.multiple_of(g * 32, 32) + j * 8, 8), :]
                high, low = split(t.reshape(128, WIDE).T)
                lh[c, g, :, j * 128 : j * 128 + 128] = high
                ll[c, g, :, j * 128 : j * 128 + 128] = low
            return 0

        lax.fori_loop(0, 4, rows, 0)

    around = ((turn(y, -1), turn(y, 1)), (turn(x, -1), turn(x, 1)))
    axes = ((x, y, x_next, x_last, y_next, y_last), (y, x, y_next, y_last, x_next, x_last))
    half_cap = cap // 2
    whole, low_part, high_part = pl.ds(0, cap), pl.ds(0, half_cap), pl.ds(half_cap, cap - half_cap)
    p1, p2 = {}, {}
    for load in small:
        load.wait()

    def line_send(h, k, n, there, part):
        b, target = axes[h][1], axes[h][2 + k % 2]

        def make():
            return remote(
                got[h][n].at[b, part], got[h][there].at[b, part], p1s.at[h, k], p1r.at[h, k], target
            )

        p1[h, k] = go(make)

    for h in range(2):
        b = axes[h][1]

        def pack(i, _):
            for u in range(8):
                got[h][0][b, i * 8 + u] = v2_ref[h, table[h, i * 8 + u]]
            return 0

        lax.fori_loop(0, cap // 8, pack, 0)
        line_send(h, 0, 0, 1, whole)
        line_send(h, 1, 0, 2, whole)

    def line_near(h):
        p1[h, 0]().wait_recv()
        line_send(h, 2, 1, 3, low_part)
        p1[h, 1]().wait_recv()
        line_send(h, 3, 2, 3, high_part)

    def plane_move(h, n, k, at, part):
        target = axes[h][4 + k % 2]

        def make():
            spot = got[h][n].at[at, part]
            return remote(spot, spot, p2s.at[h, n, k], p2r.at[h, n, k], target)

        p2[h, n, k] = go(make)

    def plane_send(h, n):
        if n == 3:
            p1[h, 2]().wait_recv()
            p1[h, 3]().wait_recv()
        plane_move(h, n, 0, axes[h][1], whole)
        plane_move(h, n, 1, axes[h][1], whole)

    def plane_near(h, n):
        p2[h, n, 0]().wait_recv()
        plane_move(h, n, 2, around[h][0], low_part)
        p2[h, n, 1]().wait_recv()
        plane_move(h, n, 3, around[h][1], high_part)

    def right(h, n):
        p2[h, n, 2]().wait_recv()
        p2[h, n, 3]().wait_recv()

        def columns(q, _):
            for j in range(4):
                tiles = []
                for kk in range(2):
                    for zz in range(4):
                        for i in range(2):
                            m = (2 * i + kk) * 4 + zz
                            t = m * HALF_BLOCKS + q
                            tiles.append(got[h][n][j, table[2 + h, t]] * table[4 + h, t].astype(F32))
                high, low = split(jnp.concatenate(tiles, axis=0))
                cut = pl.ds(pl.multiple_of(q * 128, 128), 128)
                rh[n % 2, h, j * 128 : j * 128 + 128, cut] = high
                rl[n % 2, h, j * 128 : j * 128 + 128, cut] = low
            return 0

        lax.fori_loop(0, HALF_BLOCKS, columns, 0)

    def stage0():
        for h in both:
            line_near(h)
            plane_send(h, 0)
        occupied_near(0)
        for h in both:
            plane_near(h, 0)
            plane_send(h, 1)
        occupied_far(0)
        occupied_near(1)
        left(0)
        for h in both:
            plane_near(h, 1)
            plane_send(h, 2)
        for h in both:
            right(h, 0)

    def stage1():
        occupied_far(1)
        occupied_near(2)
        left(1)

    def stage2():
        for h in both:
            plane_near(h, 2)
            plane_send(h, 3)
        for h in both:
            right(h, 1)

    def stage3():
        occupied_far(2)
        left(2)

    def stage4():
        for h in both:
            plane_near(h, 3)
        for h in both:
            right(h, 2)

    def stage5():
        for h in both:
            right(h, 3)

    both = range(2)

    def clear(i, _):
        acc[pl.ds(pl.multiple_of(i * 64, 64), 64), :] = jnp.zeros((64, 6 * WIDE), F32)
        return 0

    lax.fori_loop(0, 18, clear, 0)

    def run(s, _):
        for number, stage in enumerate((stage0, stage1, stage2, stage3, stage4, stage5)):
            pl.when(s == number)(stage)

        def multiply(t, _):
            k, h = t // 2, lax.rem(t, 2)
            i = jnp.where(s == 0, 0, jnp.where(s == 1, 1, jnp.where(s == 3, 2, k)))
            n = jnp.where(s < 2, 0, jnp.where(s == 2, 1, jnp.where(s == 3, k, s - 2)))
            shift = jnp.where(n == 0, 0, jnp.where(n == 1, 3, jnp.where(n == 2, 1, 2)))
            c = lax.rem(jnp.where(h == 0, x, y) + shift, 4)
            b = lax.rem(n, 2)
            spot = (
                pl.ds(pl.multiple_of(i * WIDE, WIDE), WIDE),
                pl.ds(pl.multiple_of(h * 3 * WIDE, 3 * WIDE), 3 * WIDE),
            )
            acc[spot] += dot3(lh[i, c], ll[i, c], rh[b, h], rl[b, h])
            return 0

        lax.fori_loop(0, 2 * jnp.where(s < 2, 1, jnp.where(s < 4, 2, 3)), multiply, 0)
        return 0

    lax.fori_loop(0, 6, run, 0)

    result = pltpu.make_async_copy(acc, out_ref, osem)
    result.start()
    for make in sent:
        make().wait_send()
    result.wait()


def spread(tile_map, three_centre, occupied, virtual):
    any_space, vmem = pl.BlockSpec(memory_space=pl.ANY), pl.BlockSpec(memory_space=pltpu.VMEM)
    dma = pltpu.SemaphoreType.DMA
    return pl.pallas_call(
        spread_kernel,
        name="spread",
        out_shape=(
            jax.ShapeDtypeStruct((2, 4, 4, HALF_BLOCKS, 8, 128), F32),
            jax.ShapeDtypeStruct((2, 3, PAIRS, WIDE), F32),
            jax.ShapeDtypeStruct((16, 8, 128), jnp.int32),
            jax.ShapeDtypeStruct((8, 8, 128), jnp.int32),
        ),
        in_specs=[any_space] * 4,
        out_specs=(any_space, any_space, vmem, vmem),
        scratch_shapes=[
            pltpu.SMEM((1, 2 * HALF_BLOCKS), jnp.int32),
            pltpu.VMEM((1024, PAIRS), F32),
            pltpu.VMEM((1024, PAIRS), F32),
            pltpu.VMEM((6, 1024, WIDE), F32),
            pltpu.VMEM((2 * PAIRS, 1024), BF16),
            pltpu.VMEM((2 * PAIRS, 1024), BF16),
            pltpu.VMEM((2, HALF_BLOCKS, PAIRS, 128), F32),
            pltpu.VMEM((2, 3, PAIRS, WIDE), F32),
            pltpu.VMEM((2, 4, HALF_BLOCKS, 32, 128), F32),
            pltpu.VMEM((4, 4, 8, 128), jnp.int32),
            pltpu.VMEM((8, 8, 128), jnp.int32),
            pltpu.VMEM((2, 3, PAIRS, WIDE), F32),
            pltpu.VMEM((2, 3, PAIRS, WIDE), F32),
            dma((3,)), dma((6,)), dma((2, 3)), dma((2, 3)), dma((2, 3)), dma((2, 3)), dma((2,)),
            dma((3, 2, 3)), dma((3, 2, 3)),
            dma((2, 3)), dma((2, 3)), dma((7,)), dma((7,)),
        ],
        compiler_params=pltpu.CompilerParams(collective_id=0, has_side_effects=True, vmem_limit_bytes=62 << 20),
    )(tile_map, three_centre, occupied, virtual)


def join(cap, number, table, v2, op):
    any_space = pl.BlockSpec(memory_space=pl.ANY)
    dma = pltpu.SemaphoreType.DMA
    return pl.pallas_call(
        functools.partial(join_kernel, cap),
        name=f"join{cap}",
        out_shape=jax.ShapeDtypeStruct((3 * WIDE, 6 * WIDE), F32),
        in_specs=[any_space] * 3,
        out_specs=any_space,
        scratch_shapes=[pltpu.SMEM((6, TILES), jnp.int32), pltpu.VMEM((2, TILES, 8, 128), F32)]
        + [pltpu.VMEM((4, cap, 8, 128), F32)] * 8
        + [
            pltpu.VMEM((3, 2, 4, 2, PAIRS, WIDE), F32),
            pltpu.VMEM((3, 4, WIDE, 512), BF16),
            pltpu.VMEM((3, 4, WIDE, 512), BF16),
            pltpu.VMEM((2, 2, 512, 3 * WIDE), BF16),
            pltpu.VMEM((2, 2, 512, 3 * WIDE), BF16),
            pltpu.VMEM((3 * WIDE, 6 * WIDE), F32),
            dma((2, 4)), dma((2, 4)), dma((2, 4, 4)), dma((2, 4, 4)),
            dma((3, 4)), dma((3, 4)), dma((3, 4)), dma((3, 4)), dma((3,)), dma, dma((2,)),
        ],
        compiler_params=pltpu.CompilerParams(
            collective_id=number, has_side_effects=True, vmem_limit_bytes=62 << 20
        ),
    )(table, v2, op)


def tables(maps, sums):
    kept = maps[:, 0, : 2 * HALF_BLOCKS].reshape(16, 2, HALF_BLOCKS).transpose(1, 0, 2).reshape(2, TILES)
    order = jnp.arange(TILES, dtype=jnp.int32)
    before = (order[None, :] < order[:, None]).astype(jnp.int32)
    pos = jnp.sum(kept[:, None, :] * before[None], axis=2) * kept
    hit = (pos[:, None, :] == order[None, :, None]) & (kept[:, None, :] == 1)
    idx = jnp.sum(jnp.where(hit, order[None, None, :], 0), axis=2)
    most = jnp.max(jnp.sum(sums[:, 0, : 2 * HALF_BLOCKS].reshape(8, 2, HALF_BLOCKS), axis=2))
    return jnp.concatenate([idx, pos, kept], axis=0), most


def body(three_centre, occupied, virtual, tile_map):
    v2, op, maps, sums = spread(tile_map, three_centre[0], occupied[0], virtual[0])
    table, most = tables(maps, sums)
    branches = [functools.partial(join, cap, i + 1) for i, cap in enumerate(CAPS)]
    chosen = sum((most > cap).astype(jnp.int32) for cap in CAPS[:-1])
    return lax.switch(chosen, branches, table, v2.reshape(2, TILES, 8, 128), op)


def solution(mesh):
    return jax.shard_map(
        body,
        mesh=mesh,
        in_specs=(
            P("row", None, "col"),
            P("row", None, None),
            P("row", None, None),
            P("row", "col"),
        ),
        out_specs=P("row", "col"),
        check_vma=False,
    )
```

time: 458 us -> 178 us (0.39)
  matrix products: 174 us -> 0 us
  Pallas kernels: 0 us -> 162 us
  blocking collectives: 130 us -> 0 us
  waiting for transfers between devices: 129 us -> 0 us
  between operations: 13.4 us -> 2.66 us
    dot_general x3 -> x0, matrix products: 174 us -> none  [the longest x1 138 us: pair_product(): lax.dot_general(left_rows, right_rows, (((0,), (0,)), ((), ())), precisio...]
    pallas_call x0 -> x2, Pallas kernels: none -> 162 us  [the longest x1 103 us: join(): pl.pallas_call(functools.partial(join_kernel, cap), name=f'join{cap}', ou...]
    all_to_all x1 -> x0, blocking collectives: 130 us -> none  [body(): lax.all_to_all(occupied_wide, 'row', split_axis=1, concat_axis=0, tiled=T...]
    all_gather x2 -> x0, waiting for transfers between devices: 129 us -> none  [the longest x1 89 us: body(): lax.all_gather(virtual_rows, 'row', axis=0, tiled=True)]
    all_to_all x1 -> x0, local copies, waits for them, and re-layouts: 9.59 us -> none  [body(): lax.all_to_all(occupied_wide, 'row', split_axis=1, concat_axis=0, tiled=T...]
    unnamed x6 -> x1, local copies, waits for them, and re-layouts: 0.27 us -> 8.83 us
  transfers between devices with their start and end apart: 2 -> 0, of which waited for: 2 -> 0; matrix products, arithmetic and copies ran while one was open for 6% -> 0% of each run, Pallas kernels for 0% -> 0%
where the time goes in v1:
time: 178 us; the launch traced here: 177 us
  Pallas kernels  162 us (91%)
  local copies, waits for them, and re-layouts  10.7 us (6%)
  between operations  2.66 us (1%)
    pallas_call x1, Pallas kernels, join(): pl.pallas_call(functools.partial(join_kernel, cap), name=f'join{cap}', ou...  103 us
    pallas_call x1, Pallas kernels, spread(): pl.pallas_call(spread_kernel, name='spread', out_shape=(jax.ShapeDtypeStr...  59 us
    unnamed x1, local copies, waits for them, and re-layouts  8.83 us

profile of v1, /device:TPU:1, one launch (start us, length us, event | category | flops | bytes accessed | tf_op | source)
XLA Modules:
  0.0 177.2 jit_solution(2284296487143710083)
XLA Ops:
  0.0 59.0 %spread.1 = (f32[2,4,4,9,8,128]{5,4,3,2,1,0:T(8,128)S(1)}, f32[2,3,128,384]{3,2,1,0:T(8,128)}, s32[16,8,128]{2,1,0:T(8,128)}, s32[8,8,128]{2,1,0:T(8,128)}) custom-call(s32[1,18]{1,0:T(1,128)} %map_hbm.1, f32[1024,2304]{1,0:T(8,128)} %bitcast.14, f32[1024,128]{1,0:T(8,128)} %bitcast.15, f32[1024,128]{1,0:T(8,128)} %bitcast.16), custom_call_target="tpu_custom_call" | custom-call | tf_op jit(solution)/shard_map/spread/pallas_call | solution.py:497
  59.1 0.8 slice_reduce_fusion.1
  59.8 0.1 reshape_squeeze.6
  59.9 0.2 reduce_sum.27
  60.1 0.6 reduce_max.9
  63.4 0.9 slice_reduce_fusion
  64.2 0.1 reshape_squeeze.7
  64.3 0.1 mul.22
  64.4 0.1 multiply_reduce_fusion
  64.6 0.1 select_reduce_fusion
  64.8 103.6 %conditional.1 = (f32[1152,2304]{1,0:T(8,128)}) conditional(s32[]{:T(128)} %clamp.3, (s32[6,144]{1,0:T(8,128)S(1)}, f32[2,4,4,9,8,128]{5,4,3,2,1,0:T(8,128)S(1)}, f32[2,3,128,384]{3,2,1,0:T(8,128)}) %tuple.20, (s32[6,144]{1,0:T(8,128)S(1)}, f32[2,4,4,9,8,128]{5,4,3,2,1,0:T(8,128)S(1)}, ...), branch_computations={%region_4.5_spmd, %region_5.6_spmd, %region_6.7_spmd, %region_7.8_... | conditional | bytes 8 | solution.py:573
  65.0 103.1 %join88.1 = f32[1152,2304]{1,0:T(8,128)} custom-call(s32[6,144]{1,0:T(8,128)S(1)} %get-tuple-element.47.table_hbm, f32[2,144,8,128]{3,2,1,0:T(8,128)S(1)} %bitcast.11, f32[2,3,128,384]{3,2,1,0:T(8,128)} %get-tuple-element.49.op_ref), custom_call_target="tpu_custom_call" | custom-call | tf_op jit(solution)/shard_map/cond/branch_2_fun/join88/pallas_call | solution.py:533
  168.4 8.8 %copy.22 = f32[1152,2304]{1,0:T(8,128)} copy(f32[1152,2304]{1,0:T(8,128)} %get-tuple-element.64) | data formatting | bytes 21233664
  (5 shorter events, 0.0 us)

commit v2 on v1

--- a/solution.py
+++ b/solution.py
@@ -50,7 +50,7 @@
 
 
 def spread_kernel(
-    map_hbm, t_ref, occ_hbm, vir_hbm, v2_ref, op_ref, maps_ref, sums_ref,
+    map_hbm, t_ref, occ_hbm, vir_hbm, v2_ref, op_ref, maps_ref, branch_ref,
     map_ref, occ_ref, vir_ref, tbuf, dh, dl, vbuf, obuf, v1, maps, sums,
     ox, oz, isem, tsem, s1, r1, s2, r2, loc, osend, orecv, ms, mr, ss, sr,
 ):
@@ -170,9 +170,7 @@
                 )
                 told[-1].start()
 
-        for q in range(3):
-            piece_start(0, h, q)
-
+        piece_start(0, h, 0)
         here = y if h else x
         sends = []
         for d in (1, 2, 3):
@@ -189,6 +187,15 @@
         first.append(sends)
         v1[h, here] = vbuf[h, :, pl.ds(pl.multiple_of(here * 32, 32), 32), :]
 
+    def advance(stage, q):
+        for i in range(2):
+            piece_arrived(stage, i, q)
+            if stage < 2:
+                piece_start(stage + 1, i, q)
+            if stage == 0 and q < 2:
+                piece_start(0, i, q + 1)
+
+    advance(0, 0)
     for copy in told[3:]:
         copy.wait_recv()
     sums[me_col] = jnp.sum(maps[...].reshape(16, 8, 128), axis=0)
@@ -222,21 +229,25 @@
         )
         copy.start()
         second.append(copy)
-
-        for q in range(3):
-            for i in range(2):
-                piece_arrived(h, i, q)
-                piece_start(h + 1, i, q)
+        if h == 0:
+            advance(0, 1)
+            advance(1, 0)
+    advance(0, 2)
+    advance(1, 1)
+    advance(1, 2)
 
     for copy in told[6:]:
         copy.wait_recv()
     maps_ref[...] = maps[...].reshape(16, 8, 128)
-    sums_ref[...] = sums[...]
+    counts = sums[...].astype(F32)
+    lane = lax.broadcasted_iota(jnp.int32, (8, 8, 128), 2)
+    halves = (lane < HALF_BLOCKS, (lane >= HALF_BLOCKS) & (lane < 2 * HALF_BLOCKS))
+    most = jnp.maximum(*(jnp.max(jnp.sum(jnp.where(half, counts, 0.0), axis=2)) for half in halves))
+    branch_ref[0] = sum((most > cap).astype(jnp.int32) for cap in CAPS[:-1])
     for copy in told:
         copy.wait_send()
-    for i in range(2):
-        for q in range(3):
-            piece_arrived(2, i, q)
+    for q in range(3):
+        advance(2, q)
     for copy in second:
         copy.wait()
     for h in range(2):
@@ -252,9 +263,9 @@
 
 
 def join_kernel(
-    cap, table_hbm, v2_hbm, op_ref, out_ref, table, v2_ref,
+    cap, table_hbm, v2_hbm, op_ref, acc_out, lh_out, ll_out, rh_out, rl_out, table, v2_ref,
     g00, g01, g02, g03, g10, g11, g12, g13, oall, lh, ll, rh, rl, acc,
-    p1s, p1r, p2s, p2r, zs, zr, bs, br, loc, osem, isem,
+    p1s, p1r, p2s, p2r, zs, zr, bs, br, loc, osem, lsem, isem,
 ):
     y, x, z, core = place()
     small = [pltpu.make_async_copy(table_hbm, table, isem.at[0]), pltpu.make_async_copy(v2_hbm, v2_ref, isem.at[1])]
@@ -281,15 +292,17 @@
 
     zslot = (z, turn(z, -1), turn(z, 1), turn(z, 2))
     zcopy, bcopy = {}, {}
-    for c in range(3):
-
-        def first(send, recv, n, target, c=c):
+
+    def occupied_send(c):
+        def first(send, recv, n, target):
             return go(lambda: remote(op_ref.at[:, c], oall.at[c, core, z], send.at[c, n], recv.at[c, n], target))
 
         zcopy[c, 0] = first(zs, zr, 0, z_next)
         zcopy[c, 1] = first(zs, zr, 1, z_last)
         bcopy[c, 0] = first(bs, br, 0, twin)
         pltpu.make_async_copy(op_ref.at[:, c], oall.at[c, core, z], loc.at[c]).start()
+
+    occupied_send(0)
 
     def relay(c, n, part, target):
         def make():
@@ -334,20 +347,41 @@
     around = ((turn(y, -1), turn(y, 1)), (turn(x, -1), turn(x, 1)))
     axes = ((x, y, x_next, x_last, y_next, y_last), (y, x, y_next, y_last, x_next, x_last))
     half_cap = cap // 2
-    whole, low_part, high_part = pl.ds(0, cap), pl.ds(0, half_cap), pl.ds(half_cap, cap - half_cap)
+    low_part, high_part = pl.ds(0, half_cap), pl.ds(half_cap, cap - half_cap)
     p1, p2 = {}, {}
     for load in small:
         load.wait()
 
-    def line_send(h, k, n, there, part):
+    parts = (low_part, high_part, high_part, low_part, low_part, high_part)
+
+    def line_move(h, k):
         b, target = axes[h][1], axes[h][2 + k % 2]
+        n, there = ((0, 1), (0, 2), (0, 1), (0, 2), (1, 3), (2, 3))[k]
 
         def make():
             return remote(
-                got[h][n].at[b, part], got[h][there].at[b, part], p1s.at[h, k], p1r.at[h, k], target
+                got[h][n].at[b, parts[k]], got[h][there].at[b, parts[k]], p1s.at[h, k], p1r.at[h, k], target
             )
 
         p1[h, k] = go(make)
+
+    def plane_move(h, n, k):
+        target = axes[h][4 + k % 2]
+        at = axes[h][1] if k < 4 else around[h][k - 4]
+
+        def make():
+            spot = got[h][n].at[at, parts[k]]
+            return remote(spot, spot, p2s.at[h, n, k], p2r.at[h, n, k], target)
+
+        p2[h, n, k] = go(make)
+
+    def line_arrived(h, *copies):
+        for k in copies:
+            p1[h, k]().wait_recv()
+
+    def plane_arrived(h, n, *copies):
+        for k in copies:
+            p2[h, n, k]().wait_recv()
 
     for h in range(2):
         b = axes[h][1]
@@ -358,40 +392,48 @@
             return 0
 
         lax.fori_loop(0, cap // 8, pack, 0)
-        line_send(h, 0, 0, 1, whole)
-        line_send(h, 1, 0, 2, whole)
-
-    def line_near(h):
-        p1[h, 0]().wait_recv()
-        line_send(h, 2, 1, 3, low_part)
-        p1[h, 1]().wait_recv()
-        line_send(h, 3, 2, 3, high_part)
-
-    def plane_move(h, n, k, at, part):
-        target = axes[h][4 + k % 2]
-
-        def make():
-            spot = got[h][n].at[at, part]
-            return remote(spot, spot, p2s.at[h, n, k], p2r.at[h, n, k], target)
-
-        p2[h, n, k] = go(make)
-
-    def plane_send(h, n):
-        if n == 3:
-            p1[h, 2]().wait_recv()
-            p1[h, 3]().wait_recv()
-        plane_move(h, n, 0, axes[h][1], whole)
-        plane_move(h, n, 1, axes[h][1], whole)
-
-    def plane_near(h, n):
-        p2[h, n, 0]().wait_recv()
-        plane_move(h, n, 2, around[h][0], low_part)
-        p2[h, n, 1]().wait_recv()
-        plane_move(h, n, 3, around[h][1], high_part)
+        for line in got[h]:
+            for j in range(4):
+                line[j, cap] = jnp.zeros((8, 128), F32)
+        line_move(h, 0)
+        line_move(h, 1)
+    for h in range(2):
+        line_move(h, 2)
+        line_move(h, 3)
+        plane_move(h, 0, 0)
+        plane_move(h, 0, 1)
+
+    both = range(2)
+
+    def early(n):
+        for h in both:
+            for k in (0, 1):
+                if n == 0:
+                    line_arrived(h, k)
+                    line_move(h, k + 4)
+                else:
+                    plane_arrived(h, n - 1, k)
+                    plane_move(h, n - 1, k + 4)
+        if n < 4:
+            for h in both:
+                plane_move(h, n, 2)
+                plane_move(h, n, 3)
+
+    def late(n):
+        for h in both:
+            if n == 0:
+                line_arrived(h, 2, 3)
+            else:
+                plane_arrived(h, n - 1, 2, 3)
+        if n < 3:
+            for h in both:
+                if n == 2:
+                    line_arrived(h, 4, 5)
+                plane_move(h, n + 1, 0)
+                plane_move(h, n + 1, 1)
 
     def right(h, n):
-        p2[h, n, 2]().wait_recv()
-        p2[h, n, 3]().wait_recv()
+        plane_arrived(h, n, 4, 5)
 
         def columns(q, _):
             for j in range(4):
@@ -401,7 +443,7 @@
                         for i in range(2):
                             m = (2 * i + kk) * 4 + zz
                             t = m * HALF_BLOCKS + q
-                            tiles.append(got[h][n][j, table[2 + h, t]] * table[4 + h, t].astype(F32))
+                            tiles.append(got[h][n][j, jnp.minimum(table[2 + h, t], cap)])
                 high, low = split(jnp.concatenate(tiles, axis=0))
                 cut = pl.ds(pl.multiple_of(q * 128, 128), 128)
                 rh[n % 2, h, j * 128 : j * 128 + 128, cut] = high
@@ -410,50 +452,80 @@
 
         lax.fori_loop(0, HALF_BLOCKS, columns, 0)
 
+    far = (turn(x, 2), turn(y, 2))
+    last_left = [
+        functools.partial(lambda h, k, src, dst: pltpu.make_async_copy(src.at[:, far[h]], dst.at[h], lsem.at[h, k]), h, k, src, dst)
+        for h in both
+        for k, (src, dst) in enumerate(((lh, lh_out), (ll, ll_out)))
+    ]
+    last_right = [
+        functools.partial(lambda k, src, dst: pltpu.make_async_copy(src.at[1], dst, osem.at[3 + k]), k, src, dst)
+        for k, (src, dst) in enumerate(((rh, rh_out), (rl, rl_out)))
+    ]
+
+    def rows_out(i):
+        rows = pl.ds(pl.multiple_of(i * WIDE, WIDE), WIDE)
+        return pltpu.make_async_copy(acc.at[rows], acc_out.at[rows], osem.at[i])
+
     def stage0():
-        for h in both:
-            line_near(h)
-            plane_send(h, 0)
+        early(0)
         occupied_near(0)
-        for h in both:
-            plane_near(h, 0)
-            plane_send(h, 1)
+        occupied_send(1)
+        late(0)
         occupied_far(0)
+        left(0)
+        early(1)
+        late(1)
         occupied_near(1)
-        left(0)
-        for h in both:
-            plane_near(h, 1)
-            plane_send(h, 2)
+        occupied_send(2)
         for h in both:
             right(h, 0)
 
     def stage1():
+        early(2)
         occupied_far(1)
-        occupied_near(2)
         left(1)
 
     def stage2():
-        for h in both:
-            plane_near(h, 2)
-            plane_send(h, 3)
+        late(2)
         for h in both:
             right(h, 1)
 
     def stage3():
+        early(3)
+        occupied_near(2)
+
+    def stage4():
+        late(3)
         occupied_far(2)
         left(2)
 
-    def stage4():
-        for h in both:
-            plane_near(h, 3)
+    def stage5():
+        early(4)
+        for copy in last_left:
+            copy().start()
+
+    def stage6():
         for h in both:
             right(h, 2)
 
-    def stage5():
+    def stage7():
+        late(4)
         for h in both:
             right(h, 3)
-
-    both = range(2)
+        for copy in last_right:
+            copy().start()
+
+    plan = (
+        (stage0, 0, 1, 0), (stage1, 1, 1, 0), (stage2, 0, 1, 1), (stage3, 1, 1, 1),
+        (stage4, 2, 1, 0), (stage5, 2, 1, 1), (stage6, 0, 3, 2), (stage7, 0, 0, 3),
+    )
+
+    def look_up(s, column):
+        value = plan[0][column]
+        for number, line in enumerate(plan):
+            value = jnp.where(s == number, line[column], value)
+        return value
 
     def clear(i, _):
         acc[pl.ds(pl.multiple_of(i * 64, 64), 64), :] = jnp.zeros((64, 6 * WIDE), F32)
@@ -462,14 +534,13 @@
     lax.fori_loop(0, 18, clear, 0)
 
     def run(s, _):
-        for number, stage in enumerate((stage0, stage1, stage2, stage3, stage4, stage5)):
-            pl.when(s == number)(stage)
+        for number, line in enumerate(plan):
+            pl.when(s == number)(line[0])
+        start, n = look_up(s, 1), look_up(s, 3)
+        shift = jnp.where(n == 0, 0, jnp.where(n == 1, 3, jnp.where(n == 2, 1, 2)))
 
         def multiply(t, _):
-            k, h = t // 2, lax.rem(t, 2)
-            i = jnp.where(s == 0, 0, jnp.where(s == 1, 1, jnp.where(s == 3, 2, k)))
-            n = jnp.where(s < 2, 0, jnp.where(s == 2, 1, jnp.where(s == 3, k, s - 2)))
-            shift = jnp.where(n == 0, 0, jnp.where(n == 1, 3, jnp.where(n == 2, 1, 2)))
+            i, h = start + t // 2, lax.rem(t, 2)
             c = lax.rem(jnp.where(h == 0, x, y) + shift, 4)
             b = lax.rem(n, 2)
             spot = (
@@ -477,18 +548,28 @@
                 pl.ds(pl.multiple_of(h * 3 * WIDE, 3 * WIDE), 3 * WIDE),
             )
             acc[spot] += dot3(lh[i, c], ll[i, c], rh[b, h], rl[b, h])
+
+            @pl.when((s == 6) & (h == 1))
+            def _():
+                rows_out(i).start()
+
             return 0
 
-        lax.fori_loop(0, 2 * jnp.where(s < 2, 1, jnp.where(s < 4, 2, 3)), multiply, 0)
+        lax.fori_loop(0, 2 * look_up(s, 2), multiply, 0)
         return 0
 
-    lax.fori_loop(0, 6, run, 0)
-
-    result = pltpu.make_async_copy(acc, out_ref, osem)
-    result.start()
+    lax.fori_loop(0, len(plan), run, 0)
+
     for make in sent:
         make().wait_send()
-    result.wait()
+    for i in range(3):
+        rows_out(i).wait()
+    for copy in last_left + last_right:
+        copy().wait()
+
+
+def finish_kernel(acc_ref, lh_ref, ll_ref, rh_ref, rl_ref, out_ref):
+    out_ref[...] = acc_ref[...] + dot3(lh_ref[0, 0], ll_ref[0, 0], rh_ref[0], rl_ref[0])
 
 
 def spread(tile_map, three_centre, occupied, virtual):
@@ -501,10 +582,10 @@
             jax.ShapeDtypeStruct((2, 4, 4, HALF_BLOCKS, 8, 128), F32),
             jax.ShapeDtypeStruct((2, 3, PAIRS, WIDE), F32),
             jax.ShapeDtypeStruct((16, 8, 128), jnp.int32),
-            jax.ShapeDtypeStruct((8, 8, 128), jnp.int32),
+            jax.ShapeDtypeStruct((1,), jnp.int32),
         ),
         in_specs=[any_space] * 4,
-        out_specs=(any_space, any_space, vmem, vmem),
+        out_specs=(any_space, any_space, vmem, pl.BlockSpec(memory_space=pltpu.SMEM)),
         scratch_shapes=[
             pltpu.SMEM((1, 2 * HALF_BLOCKS), jnp.int32),
             pltpu.VMEM((1024, PAIRS), F32),
@@ -533,11 +614,17 @@
     return pl.pallas_call(
         functools.partial(join_kernel, cap),
         name=f"join{cap}",
-        out_shape=jax.ShapeDtypeStruct((3 * WIDE, 6 * WIDE), F32),
+        out_shape=(
+            jax.ShapeDtypeStruct((3 * WIDE, 6 * WIDE), F32),
+            jax.ShapeDtypeStruct((2, 3, WIDE, 512), BF16),
+            jax.ShapeDtypeStruct((2, 3, WIDE, 512), BF16),
+            jax.ShapeDtypeStruct((2, 512, 3 * WIDE), BF16),
+            jax.ShapeDtypeStruct((2, 512, 3 * WIDE), BF16),
+        ),
         in_specs=[any_space] * 3,
-        out_specs=any_space,
-        scratch_shapes=[pltpu.SMEM((6, TILES), jnp.int32), pltpu.VMEM((2, TILES, 8, 128), F32)]
-        + [pltpu.VMEM((4, cap, 8, 128), F32)] * 8
+        out_specs=(any_space,) * 5,
+        scratch_shapes=[pltpu.SMEM((4, TILES), jnp.int32), pltpu.VMEM((2, TILES, 8, 128), F32)]
+        + [pltpu.VMEM((4, cap + 1, 8, 128), F32)] * 8
         + [
             pltpu.VMEM((3, 2, 4, 2, PAIRS, WIDE), F32),
             pltpu.VMEM((3, 4, WIDE, 512), BF16),
@@ -545,8 +632,8 @@
             pltpu.VMEM((2, 2, 512, 3 * WIDE), BF16),
             pltpu.VMEM((2, 2, 512, 3 * WIDE), BF16),
             pltpu.VMEM((3 * WIDE, 6 * WIDE), F32),
-            dma((2, 4)), dma((2, 4)), dma((2, 4, 4)), dma((2, 4, 4)),
-            dma((3, 4)), dma((3, 4)), dma((3, 4)), dma((3, 4)), dma((3,)), dma, dma((2,)),
+            dma((2, 6)), dma((2, 6)), dma((2, 4, 6)), dma((2, 4, 6)),
+            dma((3, 4)), dma((3, 4)), dma((3, 4)), dma((3, 4)), dma((3,)), dma((5,)), dma((2, 2)), dma((2,)),
         ],
         compiler_params=pltpu.CompilerParams(
             collective_id=number, has_side_effects=True, vmem_limit_bytes=62 << 20
@@ -554,23 +641,36 @@
     )(table, v2, op)
 
 
-def tables(maps, sums):
+def finish(acc, lh, ll, rh, rl):
+    tile = pl.BlockSpec((WIDE, 3 * WIDE), lambda h, i: (i, h))
+    left = pl.BlockSpec((1, 1, WIDE, 512), lambda h, i: (h, i, 0, 0))
+    right = pl.BlockSpec((1, 512, 3 * WIDE), lambda h, i: (h, 0, 0))
+    return pl.pallas_call(
+        finish_kernel,
+        name="finish",
+        grid=(2, 3),
+        out_shape=jax.ShapeDtypeStruct((3 * WIDE, 6 * WIDE), F32),
+        in_specs=[tile, left, left, right, right],
+        out_specs=tile,
+        compiler_params=pltpu.CompilerParams(vmem_limit_bytes=40 << 20),
+    )(acc, lh, ll, rh, rl)
+
+
+def tables(maps):
     kept = maps[:, 0, : 2 * HALF_BLOCKS].reshape(16, 2, HALF_BLOCKS).transpose(1, 0, 2).reshape(2, TILES)
     order = jnp.arange(TILES, dtype=jnp.int32)
     before = (order[None, :] < order[:, None]).astype(jnp.int32)
-    pos = jnp.sum(kept[:, None, :] * before[None], axis=2) * kept
-    hit = (pos[:, None, :] == order[None, :, None]) & (kept[:, None, :] == 1)
+    pos = jnp.where(kept == 1, jnp.sum(kept[:, None, :] * before[None], axis=2), TILES)
+    hit = pos[:, None, :] == order[None, :, None]
     idx = jnp.sum(jnp.where(hit, order[None, None, :], 0), axis=2)
-    most = jnp.max(jnp.sum(sums[:, 0, : 2 * HALF_BLOCKS].reshape(8, 2, HALF_BLOCKS), axis=2))
-    return jnp.concatenate([idx, pos, kept], axis=0), most
+    return jnp.concatenate([idx, pos], axis=0)
 
 
 def body(three_centre, occupied, virtual, tile_map):
-    v2, op, maps, sums = spread(tile_map, three_centre[0], occupied[0], virtual[0])
-    table, most = tables(maps, sums)
+    v2, op, maps, chosen = spread(tile_map, three_centre[0], occupied[0], virtual[0])
+    table = tables(maps)
     branches = [functools.partial(join, cap, i + 1) for i, cap in enumerate(CAPS)]
-    chosen = sum((most > cap).astype(jnp.int32) for cap in CAPS[:-1])
-    return lax.switch(chosen, branches, table, v2.reshape(2, TILES, 8, 128), op)
+    return finish(*lax.switch(chosen[0], branches, table, v2.reshape(2, TILES, 8, 128), op))
 
 
 def solution(mesh):

time: 178 us -> 156 us (0.88)
  local copies, waits for them, and re-layouts: 10.7 us -> 1.04 us
  Pallas kernels: 162 us -> 153 us
  between operations: 2.66 us -> 0.65 us
    pallas_call x0 -> x1, Pallas kernels: none -> 16 us  [finish(): pl.pallas_call(finish_kernel, name='finish', grid=(2, 3), out_shape=jax.S...]
    pallas_call x1, Pallas kernels: 103 us -> 89.5 us  [join(): pl.pallas_call(functools.partial(join_kernel, cap), name=f'join{cap}', ou...]
    pallas_call x1, Pallas kernels: 59 us -> 47.3 us  [spread(): pl.pallas_call(spread_kernel, name='spread', out_shape=(jax.ShapeDtypeStr...]
    unnamed x1 -> x0, local copies, waits for them, and re-layouts: 8.83 us -> none
where the time goes in v2:
time: 156 us
  Pallas kernels  153 us (98%)
    pallas_call x1, Pallas kernels, join(): pl.pallas_call(functools.partial(join_kernel, cap), name=f'join{cap}', ou...  89.5 us
    pallas_call x1, Pallas kernels, spread(): pl.pallas_call(spread_kernel, name='spread', out_shape=(jax.ShapeDtypeStr...  47.3 us
    pallas_call x1, Pallas kernels, finish(): pl.pallas_call(finish_kernel, name='finish', grid=(2, 3), out_shape=jax.S...  16 us

profile of v2, /device:TPU:1, one launch (start us, length us, event | category | flops | bytes accessed | tf_op | source)
XLA Modules:
  0.0 155.5 jit_solution(7252069648872550236)
XLA Ops:
  0.0 47.3 %spread.1 = (f32[2,4,4,9,8,128]{5,4,3,2,1,0:T(8,128)S(1)}, f32[2,3,128,384]{3,2,1,0:T(8,128)}, s32[16,8,128]{2,1,0:T(8,128)}, s32[1]{0:T(128)}) custom-call(s32[1,18]{1,0:T(1,128)} %map_hbm.1, f32[1024,2304]{1,0:T(8,128)} %bitcast.11, f32[1024,128]{1,0:T(8,128)} %bitcast.12, f32[1024,128]{1,0:T(8,128)} %bitcast.13), custom_call_target="tpu_custom_call" | custom-call | tf_op jit(solution)/shard_map/spread/pallas_call | solution.py:578
  47.9 0.9 slice_reduce_fusion
  48.8 0.1 reshape_squeeze.3
  48.8 0.1 reshape.31
  48.9 0.1 multiply_reduce_fusion
  49.1 0.2 select_reduce_fusion
  49.3 90.3 %conditional.1 = ((f32[1152,2304]{1,0:T(8,128)}, bf16[2,3,384,512]{3,2,1,0:T(8,128)(2,1)}, bf16[2,3,384,512]{3,2,1,0:T(8,128)(2,1)}, bf16[2,512,1152]{2,1,0:T(8,128)(2,1)}, bf16[2,512,1152]{2,1,0:T(8,128)(2,1)})) conditional(s32[]{:T(128)} %bitcast.3, (s32[4,144]{1,0:T(4,128)S(1)}, f32[2,144,8,128]{3,2,1,0:T(8,128)S(1)}, ...), branch_computations={%region_2.3_spmd, %region_3.4_spmd, %region_4.5_spmd, %region_5.6_... | conditional | bytes 8 | solution.py:673
  49.5 89.5 %join80.1 = (f32[1152,2304]{1,0:T(8,128)}, bf16[2,3,384,512]{3,2,1,0:T(8,128)(2,1)}, bf16[2,3,384,512]{3,2,1,0:T(8,128)(2,1)}, bf16[2,512,1152]{2,1,0:T(8,128)(2,1)}, bf16[2,512,1152]{2,1,0:T(8,128)(2,1)}) custom-call(s32[4,144]{1,0:T(4,128)S(1)} %get-tuple-element.38.table_hbm, f32[2,144,8,128]{3,2,1,0:T(8,128)S(1)} %get-tuple-element.39.v2_hbm, ...), custom_call_target="tpu_custom_call" | custom-call | tf_op jit(solution)/shard_map/cond/branch_1_fun/join80/pallas_call | solution.py:614
  139.6 16.0 %finish.1 = f32[1152,2304]{1,0:T(8,128)} custom-call(f32[1152,2304]{1,0:T(8,128)} %get-tuple-element.63.acc_ref, bf16[2,3,384,512]{3,2,1,0:T(8,128)(2,1)} %get-tuple-element.64.lh_ref, bf16[2,3,384,512]{3,2,1,0:T(8,128)(2,1)} %get-tuple-element.65.ll_ref, bf16[2,512,1152]{2,1,0:T(8,128)(2,1)} %get-tuple-element.66.rh_ref, ...), custom_call_target="tpu_custom_call" | custom-call | tf_op jit(solution)/shard_map/finish/pallas_call | solution.py:648
  (4 shorter events, 0.0 us)

commit v3 on v2

--- a/solution.py
+++ b/solution.py
@@ -263,16 +263,15 @@
 
 
 def join_kernel(
-    cap, table_hbm, v2_hbm, op_ref, acc_out, lh_out, ll_out, rh_out, rl_out, table, v2_ref,
-    g00, g01, g02, g03, g10, g11, g12, g13, oall, lh, ll, rh, rl, acc,
-    p1s, p1r, p2s, p2r, zs, zr, bs, br, loc, osem, lsem, isem,
+    cap, table_hbm, v2_hbm, op_ref, acc_out, lh_out, ll_out, rh_out, rl_out, table, v2_ref, *refs
 ):
+    oall, lh, ll, rh, rl, acc, p1s, p1r, p2s, p2r, zs, zr, bs, br, loc, osem, lsem, isem = refs[32:]
     y, x, z, core = place()
     small = [pltpu.make_async_copy(table_hbm, table, isem.at[0]), pltpu.make_async_copy(v2_hbm, v2_ref, isem.at[1])]
     for load in small:
         load.start()
     barrier = pltpu.get_barrier_semaphore()
-    got = ((g00, g01, g02, g03), (g10, g11, g12, g13))
+    got = [[refs[16 * h + 4 * n : 16 * h + 4 * n + 4] for n in range(4)] for h in range(2)]
     near = (
         device(y, turn(x, 1), z, core), device(y, turn(x, -1), z, core),
         device(turn(y, 1), x, z, core), device(turn(y, -1), x, z, core),
@@ -338,13 +337,12 @@
             for j in range(4):
                 t = oall[c, :, :, :, pl.ds(pl.multiple_of(g * 32, 32) + j * 8, 8), :]
                 high, low = split(t.reshape(128, WIDE).T)
-                lh[c, g, :, j * 128 : j * 128 + 128] = high
-                ll[c, g, :, j * 128 : j * 128 + 128] = low
+                lh[c, g * 4 + j] = high
+                ll[c, g * 4 + j] = low
             return 0
 
         lax.fori_loop(0, 4, rows, 0)
 
-    around = ((turn(y, -1), turn(y, 1)), (turn(x, -1), turn(x, 1)))
     axes = ((x, y, x_next, x_last, y_next, y_last), (y, x, y_next, y_last, x_next, x_last))
     half_cap = cap // 2
     low_part, high_part = pl.ds(0, half_cap), pl.ds(half_cap, cap - half_cap)
@@ -355,23 +353,24 @@
     parts = (low_part, high_part, high_part, low_part, low_part, high_part)
 
     def line_move(h, k):
-        b, target = axes[h][1], axes[h][2 + k % 2]
+        target = axes[h][2 + k % 2]
         n, there = ((0, 1), (0, 2), (0, 1), (0, 2), (1, 3), (2, 3))[k]
 
         def make():
             return remote(
-                got[h][n].at[b, parts[k]], got[h][there].at[b, parts[k]], p1s.at[h, k], p1r.at[h, k], target
+                got[h][n][0].at[parts[k]], got[h][there][0].at[parts[k]], p1s.at[h, k], p1r.at[h, k], target
             )
 
         p1[h, k] = go(make)
 
     def plane_move(h, n, k):
         target = axes[h][4 + k % 2]
-        at = axes[h][1] if k < 4 else around[h][k - 4]
+        here, there = ((0, 1), (0, 2), (0, 1), (0, 2), (1, 3), (2, 3))[k]
 
         def make():
-            spot = got[h][n].at[at, parts[k]]
-            return remote(spot, spot, p2s.at[h, n, k], p2r.at[h, n, k], target)
+            return remote(
+                got[h][n][here].at[parts[k]], got[h][n][there].at[parts[k]], p2s.at[h, n, k], p2r.at[h, n, k], target
+            )
 
         p2[h, n, k] = go(make)
 
@@ -384,17 +383,16 @@
             p2[h, n, k]().wait_recv()
 
     for h in range(2):
-        b = axes[h][1]
 
         def pack(i, _):
             for u in range(8):
-                got[h][0][b, i * 8 + u] = v2_ref[h, table[h, i * 8 + u]]
+                got[h][0][0][i * 8 + u] = v2_ref[h, table[h, i * 8 + u]]
             return 0
 
         lax.fori_loop(0, cap // 8, pack, 0)
         for line in got[h]:
-            for j in range(4):
-                line[j, cap] = jnp.zeros((8, 128), F32)
+            for packed in line:
+                packed[cap] = jnp.zeros((8, 128), F32)
         line_move(h, 0)
         line_move(h, 1)
     for h in range(2):
@@ -427,41 +425,57 @@
                 plane_arrived(h, n - 1, 2, 3)
         if n < 3:
             for h in both:
-                if n == 2:
-                    line_arrived(h, 4, 5)
                 plane_move(h, n + 1, 0)
                 plane_move(h, n + 1, 1)
 
-    def right(h, n):
-        plane_arrived(h, n, 4, 5)
+    groups = (
+        ((0, 0), (1, 0), (2, 0), (3, 0)),
+        ((0, 1), (0, 2), (1, 1), (1, 2)),
+        ((2, 1), (2, 2), (0, 3), (1, 3)),
+        ((3, 1), (3, 2), (2, 3), (3, 3)),
+    )
+
+    def right(h, g):
 
         def columns(q, _):
-            for j in range(4):
+            for j, (n, k) in enumerate(groups[g]):
                 tiles = []
                 for kk in range(2):
                     for zz in range(4):
                         for i in range(2):
                             m = (2 * i + kk) * 4 + zz
                             t = m * HALF_BLOCKS + q
-                            tiles.append(got[h][n][j, jnp.minimum(table[2 + h, t], cap)])
+                            tiles.append(got[h][n][k][jnp.minimum(table[2 + h, t], cap)])
                 high, low = split(jnp.concatenate(tiles, axis=0))
                 cut = pl.ds(pl.multiple_of(q * 128, 128), 128)
-                rh[n % 2, h, j * 128 : j * 128 + 128, cut] = high
-                rl[n % 2, h, j * 128 : j * 128 + 128, cut] = low
+                rh[g % 2, h, j * 128 : j * 128 + 128, cut] = high
+                rl[g % 2, h, j * 128 : j * 128 + 128, cut] = low
             return 0
 
         lax.fori_loop(0, HALF_BLOCKS, columns, 0)
 
-    far = (turn(x, 2), turn(y, 2))
-    last_left = [
-        functools.partial(lambda h, k, src, dst: pltpu.make_async_copy(src.at[:, far[h]], dst.at[h], lsem.at[h, k]), h, k, src, dst)
-        for h in both
-        for k, (src, dst) in enumerate(((lh, lh_out), (ll, ll_out)))
-    ]
-    last_right = [
-        functools.partial(lambda k, src, dst: pltpu.make_async_copy(src.at[1], dst, osem.at[3 + k]), k, src, dst)
-        for k, (src, dst) in enumerate(((rh, rh_out), (rl, rl_out)))
-    ]
+    def shift(k):
+        return jnp.where(k == 0, 0, jnp.where(k == 1, 3, jnp.where(k == 2, 1, 2)))
+
+    def left_at(h, n, k):
+        first, second = jnp.where(h == 0, x, y), jnp.where(h == 0, y, x)
+        return lax.rem(first + shift(n), 4) * 4 + lax.rem(second + shift(k), 4)
+
+    last_at = [[left_at(h, n, k) for n, k in groups[3]] for h in both]
+
+    def last_left():
+        return [
+            pltpu.make_async_copy(src.at[:, last_at[h][j]], dst.at[h, j], lsem.at[k, h, j])
+            for k, (src, dst) in enumerate(((lh, lh_out), (ll, ll_out)))
+            for h in both
+            for j in range(4)
+        ]
+
+    def last_right():
+        return [
+            pltpu.make_async_copy(src.at[1], dst, osem.at[3 + k])
+            for k, (src, dst) in enumerate(((rh, rh_out), (rl, rl_out)))
+        ]
 
     def rows_out(i):
         rows = pl.ds(pl.multiple_of(i * WIDE, WIDE), WIDE)
@@ -474,19 +488,20 @@
         late(0)
         occupied_far(0)
         left(0)
+        for h in both:
+            line_arrived(h, 4, 5)
+            right(h, 0)
+
+    def stage1():
         early(1)
-        late(1)
         occupied_near(1)
         occupied_send(2)
-        for h in both:
-            right(h, 0)
-
-    def stage1():
-        early(2)
+        late(1)
         occupied_far(1)
         left(1)
 
     def stage2():
+        early(2)
         late(2)
         for h in both:
             right(h, 1)
@@ -499,11 +514,14 @@
         late(3)
         occupied_far(2)
         left(2)
+        for copy in last_left():
+            copy.start()
 
     def stage5():
         early(4)
-        for copy in last_left:
-            copy().start()
+        for h in both:
+            plane_arrived(h, 0, 4, 5)
+            plane_arrived(h, 1, 4, 5)
 
     def stage6():
         for h in both:
@@ -512,9 +530,11 @@
     def stage7():
         late(4)
         for h in both:
+            plane_arrived(h, 2, 4, 5)
+            plane_arrived(h, 3, 4, 5)
             right(h, 3)
-        for copy in last_right:
-            copy().start()
+        for copy in last_right():
+            copy.start()
 
     plan = (
         (stage0, 0, 1, 0), (stage1, 1, 1, 0), (stage2, 0, 1, 1), (stage3, 1, 1, 1),
@@ -536,18 +556,25 @@
     def run(s, _):
         for number, line in enumerate(plan):
             pl.when(s == number)(line[0])
-        start, n = look_up(s, 1), look_up(s, 3)
-        shift = jnp.where(n == 0, 0, jnp.where(n == 1, 3, jnp.where(n == 2, 1, 2)))
+        start, g = look_up(s, 1), look_up(s, 3)
+        places = []
+        for j in range(4):
+            n, k = groups[0][j]
+            for number in (1, 2):
+                n = jnp.where(g == number, groups[number][j][0], n)
+                k = jnp.where(g == number, groups[number][j][1], k)
+            places.append((n, k))
 
         def multiply(t, _):
             i, h = start + t // 2, lax.rem(t, 2)
-            c = lax.rem(jnp.where(h == 0, x, y) + shift, 4)
-            b = lax.rem(n, 2)
+            rows = [left_at(h, n, k) for n, k in places]
+            b = lax.rem(g, 2)
             spot = (
                 pl.ds(pl.multiple_of(i * WIDE, WIDE), WIDE),
                 pl.ds(pl.multiple_of(h * 3 * WIDE, 3 * WIDE), 3 * WIDE),
             )
-            acc[spot] += dot3(lh[i, c], ll[i, c], rh[b, h], rl[b, h])
+            high, low = (jnp.concatenate([ref[i, r] for r in rows], axis=1) for ref in (lh, ll))
+            acc[spot] += dot3(high, low, rh[b, h], rl[b, h])
 
             @pl.when((s == 6) & (h == 1))
             def _():
@@ -564,12 +591,13 @@
         make().wait_send()
     for i in range(3):
         rows_out(i).wait()
-    for copy in last_left + last_right:
-        copy().wait()
+    for copy in last_left() + last_right():
+        copy.wait()
 
 
 def finish_kernel(acc_ref, lh_ref, ll_ref, rh_ref, rl_ref, out_ref):
-    out_ref[...] = acc_ref[...] + dot3(lh_ref[0, 0], ll_ref[0, 0], rh_ref[0], rl_ref[0])
+    high, low = (jnp.concatenate([ref[0, j, 0] for j in range(4)], axis=1) for ref in (lh_ref, ll_ref))
+    out_ref[...] = acc_ref[...] + dot3(high, low, rh_ref[0], rl_ref[0])
 
 
 def spread(tile_map, three_centre, occupied, virtual):
@@ -616,24 +644,24 @@
         name=f"join{cap}",
         out_shape=(
             jax.ShapeDtypeStruct((3 * WIDE, 6 * WIDE), F32),
-            jax.ShapeDtypeStruct((2, 3, WIDE, 512), BF16),
-            jax.ShapeDtypeStruct((2, 3, WIDE, 512), BF16),
+            jax.ShapeDtypeStruct((2, 4, 3, WIDE, 128), BF16),
+            jax.ShapeDtypeStruct((2, 4, 3, WIDE, 128), BF16),
             jax.ShapeDtypeStruct((2, 512, 3 * WIDE), BF16),
             jax.ShapeDtypeStruct((2, 512, 3 * WIDE), BF16),
         ),
         in_specs=[any_space] * 3,
         out_specs=(any_space,) * 5,
         scratch_shapes=[pltpu.SMEM((4, TILES), jnp.int32), pltpu.VMEM((2, TILES, 8, 128), F32)]
-        + [pltpu.VMEM((4, cap + 1, 8, 128), F32)] * 8
+        + [pltpu.VMEM((cap + 1, 8, 128), F32)] * 32
         + [
             pltpu.VMEM((3, 2, 4, 2, PAIRS, WIDE), F32),
-            pltpu.VMEM((3, 4, WIDE, 512), BF16),
-            pltpu.VMEM((3, 4, WIDE, 512), BF16),
+            pltpu.VMEM((3, 16, WIDE, 128), BF16),
+            pltpu.VMEM((3, 16, WIDE, 128), BF16),
             pltpu.VMEM((2, 2, 512, 3 * WIDE), BF16),
             pltpu.VMEM((2, 2, 512, 3 * WIDE), BF16),
             pltpu.VMEM((3 * WIDE, 6 * WIDE), F32),
             dma((2, 6)), dma((2, 6)), dma((2, 4, 6)), dma((2, 4, 6)),
-            dma((3, 4)), dma((3, 4)), dma((3, 4)), dma((3, 4)), dma((3,)), dma((5,)), dma((2, 2)), dma((2,)),
+            dma((3, 4)), dma((3, 4)), dma((3, 4)), dma((3, 4)), dma((3,)), dma((5,)), dma((2, 2, 4)), dma((2,)),
         ],
         compiler_params=pltpu.CompilerParams(
             collective_id=number, has_side_effects=True, vmem_limit_bytes=62 << 20
@@ -643,7 +671,7 @@
 
 def finish(acc, lh, ll, rh, rl):
     tile = pl.BlockSpec((WIDE, 3 * WIDE), lambda h, i: (i, h))
-    left = pl.BlockSpec((1, 1, WIDE, 512), lambda h, i: (h, i, 0, 0))
+    left = pl.BlockSpec((1, 4, 1, WIDE, 128), lambda h, i: (h, 0, i, 0, 0))
     right = pl.BlockSpec((1, 512, 3 * WIDE), lambda h, i: (h, 0, 0))
     return pl.pallas_call(
         finish_kernel,

time: 156 us -> 156 us (level)
  no operation moved by 1% of the time
where the time goes in v3:
time: 156 us; the launch traced here: 155 us
  Pallas kernels  153 us (98%)
    pallas_call x1, Pallas kernels, join(): pl.pallas_call(functools.partial(join_kernel, cap), name=f'join{cap}', ou...  89.3 us
    pallas_call x1, Pallas kernels, spread(): pl.pallas_call(spread_kernel, name='spread', out_shape=(jax.ShapeDtypeStr...  47.3 us
    pallas_call x1, Pallas kernels, finish(): pl.pallas_call(finish_kernel, name='finish', grid=(2, 3), out_shape=jax.S...  16 us

profile of v3, /device:TPU:1, one launch (start us, length us, event | category | flops | bytes accessed | tf_op | source)
XLA Modules:
  0.0 155.3 jit_solution(17762143404679036337)
XLA Ops:
  0.0 47.3 %spread.1 = (f32[2,4,4,9,8,128]{5,4,3,2,1,0:T(8,128)S(1)}, f32[2,3,128,384]{3,2,1,0:T(8,128)}, s32[16,8,128]{2,1,0:T(8,128)}, s32[1]{0:T(128)}) custom-call(s32[1,18]{1,0:T(1,128)} %map_hbm.1, f32[1024,2304]{1,0:T(8,128)} %bitcast.11, f32[1024,128]{1,0:T(8,128)} %bitcast.12, f32[1024,128]{1,0:T(8,128)} %bitcast.13), custom_call_target="tpu_custom_call" | custom-call | tf_op jit(solution)/shard_map/spread/pallas_call | solution.py:606
  47.9 0.9 slice_reduce_fusion
  48.8 0.1 reshape_squeeze.3
  48.8 0.1 reshape.31
  48.9 0.1 multiply_reduce_fusion
  49.1 0.2 select_reduce_fusion
  49.3 90.1 %conditional.1 = ((f32[1152,2304]{1,0:T(8,128)}, bf16[2,4,3,384,128]{4,3,2,1,0:T(8,128)(2,1)}, bf16[2,4,3,384,128]{4,3,2,1,0:T(8,128)(2,1)}, bf16[2,512,1152]{2,1,0:T(8,128)(2,1)}, bf16[2,512,1152]{2,1,0:T(8,128)(2,1)})) conditional(s32[]{:T(128)} %bitcast.3, (s32[4,144]{1,0:T(4,128)S(1)}, ...), branch_computations={%region_2.3_spmd, %region_3.4_spmd, %region_4.5_spmd, %region_5.6_... | conditional | bytes 8 | solution.py:701
  49.5 89.3 %join80.1 = (f32[1152,2304]{1,0:T(8,128)}, bf16[2,4,3,384,128]{4,3,2,1,0:T(8,128)(2,1)}, bf16[2,4,3,384,128]{4,3,2,1,0:T(8,128)(2,1)}, bf16[2,512,1152]{2,1,0:T(8,128)(2,1)}, bf16[2,512,1152]{2,1,0:T(8,128)(2,1)}) custom-call(s32[4,144]{1,0:T(4,128)S(1)} %get-tuple-element.38.table_hbm, f32[2,144,8,128]{3,2,1,0:T(8,128)S(1)} %get-tuple-element.39.v2_hbm, ...), custom_call_target="tpu_custom_call" | custom-call | tf_op jit(solution)/shard_map/cond/branch_1_fun/join80/pallas_call | solution.py:642
  139.4 16.0 %finish.1 = f32[1152,2304]{1,0:T(8,128)} custom-call(f32[1152,2304]{1,0:T(8,128)} %get-tuple-element.63.acc_ref, bf16[2,4,3,384,128]{4,3,2,1,0:T(8,128)(2,1)} %get-tuple-element.64.lh_ref, bf16[2,4,3,384,128]{4,3,2,1,0:T(8,128)(2,1)} %get-tuple-element.65.ll_ref, bf16[2,512,1152]{2,1,0:T(8,128)(2,1)} %get-tuple-element.66.rh_ref, ...), custom_call_target="tpu_custom_call" | custom-call | tf_op jit(solution)/shard_map/finish/pallas_call | solution.py:676
  (4 shorter events, 0.0 us)

commit v4 on v3

--- a/solution.py
+++ b/solution.py
@@ -13,7 +13,7 @@
 TILES = 16 * HALF_BLOCKS
 WIDE = 384
 PAIRS = 128
-CAPS = (72, 80, 88, 96, TILES)
+CAPS = (72, 76, 80, 84, 88, 96, TILES)
 
 
 def place():
@@ -171,6 +171,7 @@
                 told[-1].start()
 
         piece_start(0, h, 0)
+        piece_start(0, h, 1)
         here = y if h else x
         sends = []
         for d in (1, 2, 3):
@@ -192,8 +193,8 @@
             piece_arrived(stage, i, q)
             if stage < 2:
                 piece_start(stage + 1, i, q)
-            if stage == 0 and q < 2:
-                piece_start(0, i, q + 1)
+            if stage == 0 and q == 0:
+                piece_start(0, i, 2)
 
     advance(0, 0)
     for copy in told[3:]:
@@ -385,11 +386,11 @@
     for h in range(2):
 
         def pack(i, _):
-            for u in range(8):
-                got[h][0][0][i * 8 + u] = v2_ref[h, table[h, i * 8 + u]]
+            for u in range(4):
+                got[h][0][0][i * 4 + u] = v2_ref[h, table[h, i * 4 + u]]
             return 0
 
-        lax.fori_loop(0, cap // 8, pack, 0)
+        lax.fori_loop(0, cap // 4, pack, 0)
         for line in got[h]:
             for packed in line:
                 packed[cap] = jnp.zeros((8, 128), F32)

time: 156 us -> 151 us (0.968)
  Pallas kernels: 153 us -> 148 us
    pallas_call x1, Pallas kernels: 89.3 us -> 83 us  [join(): pl.pallas_call(functools.partial(join_kernel, cap), name=f'join{cap}', ou...]
    pallas_call x1, Pallas kernels: 47.3 us -> 49.3 us  [spread(): pl.pallas_call(spread_kernel, name='spread', out_shape=(jax.ShapeDtypeStr...]
where the time goes in v4:
time: 151 us
  Pallas kernels  148 us (98%)
    pallas_call x1, Pallas kernels, join(): pl.pallas_call(functools.partial(join_kernel, cap), name=f'join{cap}', ou...  83 us
    pallas_call x1, Pallas kernels, spread(): pl.pallas_call(spread_kernel, name='spread', out_shape=(jax.ShapeDtypeStr...  49.3 us
    pallas_call x1, Pallas kernels, finish(): pl.pallas_call(finish_kernel, name='finish', grid=(2, 3), out_shape=jax.S...  16 us

profile of v4, /device:TPU:1, one launch (start us, length us, event | category | flops | bytes accessed | tf_op | source)
XLA Modules:
  0.0 150.8 jit_solution(15120133603632823036)
XLA Ops:
  0.0 49.3 %spread.1 = (f32[2,4,4,9,8,128]{5,4,3,2,1,0:T(8,128)S(1)}, f32[2,3,128,384]{3,2,1,0:T(8,128)}, s32[16,8,128]{2,1,0:T(8,128)}, s32[1]{0:T(128)}) custom-call(s32[1,18]{1,0:T(1,128)} %map_hbm.1, f32[1024,2304]{1,0:T(8,128)} %bitcast.13, f32[1024,128]{1,0:T(8,128)} %bitcast.14, f32[1024,128]{1,0:T(8,128)} %bitcast.15), custom_call_target="tpu_custom_call" | custom-call | tf_op jit(solution)/shard_map/spread/pallas_call | solution.py:607
  49.9 0.9 slice_reduce_fusion
  50.8 0.1 reshape_squeeze.3
  50.9 0.1 reshape.31
  50.9 0.1 multiply_reduce_fusion
  51.1 0.2 select_reduce_fusion
  51.3 83.5 %conditional.1 = ((f32[1152,2304]{1,0:T(8,128)}, bf16[2,4,3,384,128]{4,3,2,1,0:T(8,128)(2,1)}, bf16[2,4,3,384,128]{4,3,2,1,0:T(8,128)(2,1)}, bf16[2,512,1152]{2,1,0:T(8,128)(2,1)}, bf16[2,512,1152]{2,1,0:T(8,128)(2,1)})) conditional(s32[]{:T(128)} %bitcast.3, (s32[4,144]{1,0:T(4,128)S(1)}, ...), branch_computations={%region_2.3_spmd, %region_3.4_spmd, %region_4.5_spmd, %region_5.6_... | conditional | bytes 8 | solution.py:702
  51.5 83.0 %join88.1 = (f32[1152,2304]{1,0:T(8,128)}, bf16[2,4,3,384,128]{4,3,2,1,0:T(8,128)(2,1)}, bf16[2,4,3,384,128]{4,3,2,1,0:T(8,128)(2,1)}, bf16[2,512,1152]{2,1,0:T(8,128)(2,1)}, bf16[2,512,1152]{2,1,0:T(8,128)(2,1)}) custom-call(s32[4,144]{1,0:T(4,128)S(1)} %get-tuple-element.59.table_hbm, f32[2,144,8,128]{3,2,1,0:T(8,128)S(1)} %get-tuple-element.60.v2_hbm, ...), custom_call_target="tpu_custom_call" | custom-call | tf_op jit(solution)/shard_map/cond/branch_4_fun/join88/pallas_call | solution.py:643
  134.8 16.0 %finish.1 = f32[1152,2304]{1,0:T(8,128)} custom-call(f32[1152,2304]{1,0:T(8,128)} %get-tuple-element.81.acc_ref, bf16[2,4,3,384,128]{4,3,2,1,0:T(8,128)(2,1)} %get-tuple-element.82.lh_ref, bf16[2,4,3,384,128]{4,3,2,1,0:T(8,128)(2,1)} %get-tuple-element.83.ll_ref, bf16[2,512,1152]{2,1,0:T(8,128)(2,1)} %get-tuple-element.84.rh_ref, ...), custom_call_target="tpu_custom_call" | custom-call | tf_op jit(solution)/shard_map/finish/pallas_call | solution.py:677
  (4 shorter events, 0.0 us)
